TPU v7x, 256 devices: a whole 4x4x8 slice. The times are simulated.
256 devices in a mesh: dom: 32 (over y_hi, z, core), col: 8 (over x, y_lo).
Axes of the slice: x: 4, y: 4 (y_hi: 2, y_lo: 2; y = y_hi * 2 + y_lo), z: 8, core: 2. Of those that a mesh axis runs over, the one named last changes fastest.
Arguments:
- tmat: bfloat16 [131072, 4096], P('dom', 'col'), may hold values from -6 to 6
- stored_mass_blocks: bfloat16 [8192, 128, 128], P('dom'), may hold values from -0.0007324219 to 0.0007324219
- block_index: int32 [8192, 2], P('dom'), may hold values from 0 to 35, as said below
- live_block_count: int32 [32], P('dom'), may hold values from 36 to 256, as said below
- send_rows: int32 [64, 256], P('dom'), may hold values from 0 to 4095, as said below
Outputs:
- reduced: float32 [512, 4096], P('dom', 'col')
Inputs may be any that keep to these rules, and one draw needn't show every extreme that they name: `block_index`: row entries lie in 0 to 31 and column entries in 0 to 35. In each partition's list slot k < 32 is block (k, k), and slot 32 + m for m < 4 has block column 32 + m. `live_block_count`: some partition uses all 256 slots in every draw. `send_rows`: the 256 rows in each list are distinct local row numbers of the sending partition.
All inputs are finite; a program needn't handle non-finite values.
Results may differ from a plain program's by a relative error of at most 0.0029.
Values may be sent and summed in bfloat16 or wider, within the bound.
A program may use at most 128 MiB of HBM per device.

v0:
```python
import jax
import jax.numpy as jnp
from jax import lax
from jax.sharding import PartitionSpec as P


def passed_along(block, axis, distance):
    devices = range(lax.axis_size(axis))
    route = [(i - distance, i) for i in devices if i - distance in devices]
    return lax.ppermute(block, axis, route)


def broadcast(block, axis, holder):
    block = jnp.where(lax.axis_index(axis) == holder, block, jnp.zeros_like(block))
    return lax.psum(block, axis)


def contract(left, right):
    return lax.dot_general(
        left, right, (((0,), (0,)), ((), ())), preferred_element_type=jnp.float32
    )


def mass_product(panel, stored_mass_blocks, block_index, live_block_count, send_rows):
    rows_dev, width = panel.shape
    bsize = stored_mass_blocks.shape[1]
    nrows_blk = rows_dev // bsize
    slot_number = stored_mass_blocks.shape[0]
    to_lower = jnp.take(panel, send_rows[0], axis=0)
    to_upper = jnp.take(panel, send_rows[1], axis=0)
    from_lower = passed_along(to_upper, "dom", 1)
    from_upper = passed_along(to_lower, "dom", -1)
    extended = jnp.concatenate([panel, from_lower, from_upper], 0).reshape(-1, bsize, width)
    live_flags = (jnp.arange(slot_number) < live_block_count[0]).astype(jnp.float32)
    partition_groups = 4
    partition_group_width = slot_number // partition_groups

    def step(acc, group):
        begin = group * partition_group_width
        blocks = lax.dynamic_slice_in_dim(stored_mass_blocks, begin, partition_group_width, 0)
        columns = lax.dynamic_slice_in_dim(block_index[:, 1], begin, partition_group_width, 0)
        targets = lax.dynamic_slice_in_dim(block_index[:, 0], begin, partition_group_width, 0)
        weights = lax.dynamic_slice_in_dim(live_flags, begin, partition_group_width, 0)
        selected = jnp.take(extended, columns, axis=0)
        prod = jnp.einsum("kab,kbw->kaw", blocks, selected, preferred_element_type=jnp.float32)
        acc = acc.at[targets].add(prod * weights[:, None, None])
        return (acc, None)

    start_acc = jnp.zeros((nrows_blk, bsize, width), jnp.float32)
    summed, _ = lax.scan(step, start_acc, jnp.arange(partition_groups))
    return summed.reshape(rows_dev, width).astype(jnp.bfloat16)


def body(tmat, stored_mass_blocks, block_index, live_block_count, send_rows):
    n_col = lax.axis_size("col")
    n_dom = lax.axis_size("dom")
    panel_width = tmat.shape[1]
    panel = broadcast(tmat, "col", n_col - 1)
    interface_mass_panel = mass_product(
        panel, stored_mass_blocks, block_index, live_block_count, send_rows
    )
    share = panel_width // n_dom
    total = lax.psum(contract(interface_mass_panel, tmat), "dom")
    return lax.dynamic_slice_in_dim(total, lax.axis_index("dom") * share, share, 0)


def solution(mesh):
    return jax.shard_map(
        body,
        mesh=mesh,
        in_specs=(P("dom", "col"), P("dom", None, None), P("dom", None), P("dom"), P("dom", None)),
        out_specs=P("dom", "col"),
        check_vma=False,
    )
```

profile of v0, /device:TPU:1, one launch (start us, length us, event | category | flops | bytes accessed | tf_op | source)
XLA Modules:
  0.0 749.2 jit_solution(13269119770228952049)
XLA Ops:
  6.5 2.2 broadcast_select_fusion
  8.8 0.0 all-reduce.3.cloned.1.call-update
  8.8 0.0 all-reduce.5.cloned.1.call-start
  9.0 192.5 %all-reduce.3.cloned.1.call-done = bf16[4096,512]{1,0:T(8,128)(2,1)} async-done(((bf16[4096,512]{1,0:T(8,128)(2,1)}), bf16[4096,512]{1,0:T(8,128)(2,1)}) %all-reduce.3.cloned.1.call-update) | async-done | bytes 4194320 | tf_op jit(solution)/shard_map/psum | solution.py:15
  201.5 3.9 gather_fusion.1
  205.4 0.1 broadcast_select_fusion.2
  205.5 3.7 collective-permute-start
  209.3 3.9 gather_fusion.2
  213.2 0.1 broadcast_select_fusion.1
  213.3 1.9 collective-permute-start.1
  216.0 5.1 collective-permute-done.1
  221.0 4.0 pad_maximum_fusion
  225.0 4.3 broadcast_in_dim.27
  229.3 233.0 %while.10 = (s32[]{:T(128)}, f32[32,128,512]{2,1,0:T(8,128)}, s32[256,2]{0,1:T(2,128)S(1)}, s32[4]{0:T(128)S(1)}, bf16[256,128,128]{2,1,0:T(8,128)(2,1)}, /*inde...) while((s32[]{:T(128)}, f32[32,128,512]{2,1,0:T(8,128)}, ...), condition=%wide.region_3.5_spmd, body=%wide.region_1.0_spmd.sunk | while | flops 1086326400 | bytes 94382912 | solution.py:50
  229.3 0.7 dynamic_slice.38
  230.7 0.1 dynamic_slice.39
  230.8 0.1 fusion.19
  230.9 0.1 and_bitcast_fusion.2
  230.9 7.9 %gather_fusion = bf16[64,128,512]{2,1,0:T(8,128)(2,1)} fusion(bf16[36,128,512]{2,1,0:T(8,128)(2,1)} %get-tuple-element.142, s32[1024]{0:T(1024)S(1)} %pad_clamp_fusion.4), kind=kCustom, calls=%fused_computation.1.clone.1 | custom fusion | bytes 16777472 | tf_op jit(solution)/shard_map/while/body/eval_jaxpr/jit(_take)/gather | solution.py:44
  238.8 12.2 %convolution_multiply_fusion.2 = f32[64,128,512]{2,1,0:T(8,128)} fusion(f32[64]{0:T(128)S(1)} %dynamic_slice.39, bf16[64,128,512]{2,1,0:T(8,128)(2,1)} %gather_fusion, pred[64]{0:T(512)(128)(4,1)S(1)} %get-tuple-element.114, bf16[256,128,128]{2,1,0:T(8,128)(2,1)} %get-tuple-element.141, s32[]{:T(128)S(6)} %select_n.70), kind=kOutput, calls=%fused_computation.4.clone.1 | convolution fusion | flops 1082130432 | bytes 27263300 | tf_op jit(solution)/shard_map/while/body/eval_jaxpr/kab,kbw->kaw/dot_general | solution.py:45
  251.0 36.9 %scatter_fusion = f32[32,128,512]{2,1,0:T(8,128)} fusion(f32[32,128,512]{2,1,0:T(8,128)} %get-tuple-element.127, s32[64]{0:T(128)S(1)} %fusion.19, f32[64,128,512]{2,1,0:T(8,128)} %convolution_multiply_fusion.2), kind=kCustom, calls=%fused_computation.3.clone.1 | custom fusion | flops 4194304 | bytes 50331904 | tf_op jit(solution)/shard_map/while/body/eval_jaxpr/scatter-add | solution.py:46
  287.9 0.7 dynamic_slice.38
  289.3 0.1 dynamic_slice.39
  289.4 0.1 fusion.19
  289.4 0.1 and_bitcast_fusion.2
  289.5 7.9 %gather_fusion = bf16[64,128,512]{2,1,0:T(8,128)(2,1)} fusion(bf16[36,128,512]{2,1,0:T(8,128)(2,1)} %get-tuple-element.142, s32[1024]{0:T(1024)S(1)} %pad_clamp_fusion.4), kind=kCustom, calls=%fused_computation.1.clone.1 | custom fusion | bytes 16777472 | tf_op jit(solution)/shard_map/while/body/eval_jaxpr/jit(_take)/gather | solution.py:44
  297.4 12.2 %convolution_multiply_fusion.2 = f32[64,128,512]{2,1,0:T(8,128)} fusion(f32[64]{0:T(128)S(1)} %dynamic_slice.39, bf16[64,128,512]{2,1,0:T(8,128)(2,1)} %gather_fusion, pred[64]{0:T(512)(128)(4,1)S(1)} %get-tuple-element.114, bf16[256,128,128]{2,1,0:T(8,128)(2,1)} %get-tuple-element.141, s32[]{:T(128)S(6)} %select_n.70), kind=kOutput, calls=%fused_computation.4.clone.1 | convolution fusion | flops 1082130432 | bytes 27263300 | tf_op jit(solution)/shard_map/while/body/eval_jaxpr/kab,kbw->kaw/dot_general | solution.py:45
  309.5 36.7 %scatter_fusion = f32[32,128,512]{2,1,0:T(8,128)} fusion(f32[32,128,512]{2,1,0:T(8,128)} %get-tuple-element.127, s32[64]{0:T(128)S(1)} %fusion.19, f32[64,128,512]{2,1,0:T(8,128)} %convolution_multiply_fusion.2), kind=kCustom, calls=%fused_computation.3.clone.1 | custom fusion | flops 4194304 | bytes 50331904 | tf_op jit(solution)/shard_map/while/body/eval_jaxpr/scatter-add | solution.py:46
  346.2 0.7 dynamic_slice.38
  347.6 0.1 dynamic_slice.39
  347.7 0.1 fusion.19
  347.7 0.1 and_bitcast_fusion.2
  347.8 7.9 %gather_fusion = bf16[64,128,512]{2,1,0:T(8,128)(2,1)} fusion(bf16[36,128,512]{2,1,0:T(8,128)(2,1)} %get-tuple-element.142, s32[1024]{0:T(1024)S(1)} %pad_clamp_fusion.4), kind=kCustom, calls=%fused_computation.1.clone.1 | custom fusion | bytes 16777472 | tf_op jit(solution)/shard_map/while/body/eval_jaxpr/jit(_take)/gather | solution.py:44
  355.7 12.2 %convolution_multiply_fusion.2 = f32[64,128,512]{2,1,0:T(8,128)} fusion(f32[64]{0:T(128)S(1)} %dynamic_slice.39, bf16[64,128,512]{2,1,0:T(8,128)(2,1)} %gather_fusion, pred[64]{0:T(512)(128)(4,1)S(1)} %get-tuple-element.114, bf16[256,128,128]{2,1,0:T(8,128)(2,1)} %get-tuple-element.141, s32[]{:T(128)S(6)} %select_n.70), kind=kOutput, calls=%fused_computation.4.clone.1 | convolution fusion | flops 1082130432 | bytes 27263300 | tf_op jit(solution)/shard_map/while/body/eval_jaxpr/kab,kbw->kaw/dot_general | solution.py:45
  367.8 36.4 %scatter_fusion = f32[32,128,512]{2,1,0:T(8,128)} fusion(f32[32,128,512]{2,1,0:T(8,128)} %get-tuple-element.127, s32[64]{0:T(128)S(1)} %fusion.19, f32[64,128,512]{2,1,0:T(8,128)} %convolution_multiply_fusion.2), kind=kCustom, calls=%fused_computation.3.clone.1 | custom fusion | flops 4194304 | bytes 50331904 | tf_op jit(solution)/shard_map/while/body/eval_jaxpr/scatter-add | solution.py:46
  404.3 0.7 dynamic_slice.38
  405.6 0.1 dynamic_slice.39
  405.7 0.1 fusion.19
  405.8 0.1 and_bitcast_fusion.2
  405.9 7.9 %gather_fusion = bf16[64,128,512]{2,1,0:T(8,128)(2,1)} fusion(bf16[36,128,512]{2,1,0:T(8,128)(2,1)} %get-tuple-element.142, s32[1024]{0:T(1024)S(1)} %pad_clamp_fusion.4), kind=kCustom, calls=%fused_computation.1.clone.1 | custom fusion | bytes 16777472 | tf_op jit(solution)/shard_map/while/body/eval_jaxpr/jit(_take)/gather | solution.py:44
  413.7 12.2 %convolution_multiply_fusion.2 = f32[64,128,512]{2,1,0:T(8,128)} fusion(f32[64]{0:T(128)S(1)} %dynamic_slice.39, bf16[64,128,512]{2,1,0:T(8,128)(2,1)} %gather_fusion, pred[64]{0:T(512)(128)(4,1)S(1)} %get-tuple-element.114, bf16[256,128,128]{2,1,0:T(8,128)(2,1)} %get-tuple-element.141, s32[]{:T(128)S(6)} %select_n.70), kind=kOutput, calls=%fused_computation.4.clone.1 | convolution fusion | flops 1082130432 | bytes 27263300 | tf_op jit(solution)/shard_map/while/body/eval_jaxpr/kab,kbw->kaw/dot_general | solution.py:45
  425.9 36.4 %scatter_fusion = f32[32,128,512]{2,1,0:T(8,128)} fusion(f32[32,128,512]{2,1,0:T(8,128)} %get-tuple-element.127, s32[64]{0:T(128)S(1)} %fusion.19, f32[64,128,512]{2,1,0:T(8,128)} %convolution_multiply_fusion.2), kind=kCustom, calls=%fused_computation.3.clone.1 | custom fusion | flops 4194304 | bytes 50331904 | tf_op jit(solution)/shard_map/while/body/eval_jaxpr/scatter-add | solution.py:46
  462.3 4.2 convert_element_type.10
  466.5 0.4 copy-done
  466.9 3.4 fusion.9
  470.3 0.0 all-reduce.5.cloned.1.call-update
  470.3 270.7 %all-reduce.5.cloned.1.call-done = f32[512,512]{1,0:T(8,128)} async-done(((f32[512,512]{1,0:T(8,128)}), f32[512,512]{1,0:T(8,128)}) %all-reduce.5.cloned.1.call-update) | async-done | bytes 1048592 | tf_op jit(solution)/shard_map/psum | solution.py:63
  741.0 1.4 constant_dynamic-slice_fusion.2
  (24 shorter events, 0.1 us)
Async XLA Ops:
  6.5 2.3 copy-start.2
  6.5 195.0 %all-reduce.3.cloned.1.call-start = ((), (), s32[]{:S(2)}) async-start(), calls=%async_computation | async-start | bytes 8388608 | tf_op jit(solution)/shard_map/psum | solution.py:15
  8.8 732.1 %all-reduce.5.cloned.1.call-start = ((), (), s32[]{:S(2)}) async-start(), calls=%async_computation.1 | async-start | bytes 2097152 | tf_op jit(solution)/shard_map/psum | solution.py:63
  205.5 10.4 %collective-permute-start = (bf16[256,512]{1,0:T(8,128)(2,1)S(1)}, bf16[256,512]{1,0:T(8,128)(2,1)S(1)}, u32[]{:S(2)}, u32[]{:S(2)}) collective-permute-start(bf16[256,512]{1,0:T(8,128)(2,1)S(1)} %broadcast_select_fusion.2), channel_id=1, source_target_pairs={{0,8},{8,16},{16,24},{24,32},{32,40},{40,48},{48,56},{56,64},{64,7... | collective-permute-start | bytes 786440 | tf_op jit(solution)/shard_map/ppermute | solution.py:10
  213.3 7.7 %collective-permute-start.1 = (bf16[256,512]{1,0:T(8,128)(2,1)S(1)}, bf16[256,512]{1,0:T(8,128)(2,1)S(1)}, u32[]{:S(2)}, u32[]{:S(2)}) collective-permute-start(bf16[256,512]{1,0:T(8,128)(2,1)S(1)} %broadcast_select_fusion.1), channel_id=1, source_target_pairs={{8,0},{16,8},{24,16},{32,24},{40,32},{48,40},{56,48},{64,56},{72,6... | collective-permute-start | bytes 786440 | tf_op jit(solution)/shard_map/ppermute | solution.py:10
  215.9 13.4 %copy-start.1 = (s32[256,2]{0,1:T(2,128)S(1)}, s32[256,2]{0,1:T(2,128)}, u32[]{:S(2)}) copy-start(s32[256,2]{0,1:T(2,128)} %param.11) | copy-start | bytes 6148
  462.3 4.6 copy-start
Sparse Core Ops, SparseCore 0:
  10.0 191.4 all-reduce.2
  470.4 270.5 all-reduce.4
where the time goes:
time: 750 us; the launch traced here: 749 us
  waiting for transfers between devices  468 us (62%)
  other arithmetic  158 us (21%)
  matrix products  52 us (7%)
  local copies, waits for them, and re-layouts  48.4 us (6%)
  between operations  14.2 us (2%)
    psum x1, waiting for transfers between devices, body(): total = lax.psum(contract(interface_mass_panel, tmat), 'dom')  271 us
    psum x1, waiting for transfers between devices, broadcast(): return lax.psum(block, axis)  193 us
    scatter-add x4, other arithmetic, step(): acc = acc.at[targets].add(prod * weights[:, None, None])  146 us
    dot_general x4, matrix products, step(): jnp.einsum('kab,kbw->kaw', blocks, selected, preferred_element_type=jnp.f...  48.6 us
    gather x4, local copies, waits for them, and re-layouts, step(): selected = jnp.take(extended, columns, axis=0)  31.5 us
  transfers between devices with their start and end apart: 4, of which 3 were waited for; matrix products, arithmetic and copies ran while one was open for 1% of the time, Pallas kernels for 0%

commit v1 on v0

--- a/solution.py
+++ b/solution.py
@@ -12,7 +12,7 @@
 
 def broadcast(block, axis, holder):
     block = jnp.where(lax.axis_index(axis) == holder, block, jnp.zeros_like(block))
-    return lax.psum(block, axis)
+    return jnp.sum(lax.all_gather(block, axis), axis=0)
 
 
 def contract(left, right):

time: 750 us -> 1220 us (1.63)
  waiting for transfers between devices: 468 us -> 923 us
  other arithmetic: 158 us -> 172 us
    all_gather x0 -> x1, waiting for transfers between devices: none -> 648 us  [broadcast(): return jnp.sum(lax.all_gather(block, axis), axis=0)]
    psum x1 -> x0, waiting for transfers between devices: 193 us -> none  [broadcast(): return lax.psum(block, axis)]
    reduce_sum x0 -> x1, other arithmetic: none -> 14.1 us  [broadcast(): return jnp.sum(lax.all_gather(block, axis), axis=0)]
  transfers between devices with their start and end apart: 4 -> 4, of which waited for: 3 -> 4; matrix products, arithmetic and copies ran while one was open for 1% -> 0% of each run, Pallas kernels for 0% -> 0%
where the time goes in v1:
time: 1220 us
  waiting for transfers between devices  923 us (76%)
  other arithmetic  172 us (14%)
  matrix products  52.1 us (4%)
  local copies, waits for them, and re-layouts  48.8 us (4%)
  between operations  14.2 us (1%)
    all_gather x1, waiting for transfers between devices, broadcast(): return jnp.sum(lax.all_gather(block, axis), axis=0)  648 us
    psum x1, waiting for transfers between devices, body(): total = lax.psum(contract(interface_mass_panel, tmat), 'dom')  270 us
    scatter-add x4, other arithmetic, step(): acc = acc.at[targets].add(prod * weights[:, None, None])  146 us
    dot_general x4, matrix products, step(): jnp.einsum('kab,kbw->kaw', blocks, selected, preferred_element_type=jnp.f...  48.7 us
    gather x4, local copies, waits for them, and re-layouts, step(): selected = jnp.take(extended, columns, axis=0)  31.9 us
  transfers between devices with their start and end apart: 4, of which 4 were waited for; matrix products, arithmetic and copies ran while one was open for 0% of the time, Pallas kernels for 0%

profile of v1, /device:TPU:1, one launch (start us, length us, event | category | flops | bytes accessed | tf_op | source)
XLA Modules:
  0.0 1218.2 jit_solution(2729107689817956845)
XLA Ops:
  6.5 2.2 broadcast_select_fusion
  8.8 0.0 all-reduce.2.cloned.1.call-start
  8.9 648.4 %all-gather.3.cloned.1.call-done = bf16[32768,512]{1,0:T(8,128)(2,1)} async-done(((bf16[4096,512]{1,0:T(8,128)(2,1)}), bf16[32768,512]{1,0:T(8,128)(2,1)}) %all-gather.3.cloned.1.call-update) | async-done | bytes 33554448 | tf_op jit(solution)/shard_map/all_gather | solution.py:15
  657.3 14.1 %reduce_sum.12 = bf16[4096,512]{1,0:T(8,128)(2,1)} reduce(bf16[8,4096,512]{2,1,0:T(8,128)(2,1)} %bitcast.24, bf16[]{:T(256)} %constant.59.clone.1), dimensions={0}, to_apply=%region_0.1 | reduce | flops 14680064 | bytes 37748736 | tf_op jit(solution)/shard_map/reduce_sum | solution.py:15
  671.4 3.9 gather_fusion.2
  675.3 3.9 gather_fusion.1
  679.2 0.1 broadcast_select_fusion.2
  679.4 3.7 collective-permute-start
  683.1 0.1 broadcast_select_fusion.1
  683.2 2.1 collective-permute-start.1
  686.0 0.4 collective-permute-done
  686.4 4.5 collective-permute-done.1
  690.9 3.9 pad_maximum_fusion
  694.8 4.3 broadcast_in_dim.27
  699.1 233.3 %while.10 = (s32[]{:T(128)}, f32[32,128,512]{2,1,0:T(8,128)}, s32[256,2]{0,1:T(2,128)S(1)}, s32[4]{0:T(128)S(1)}, bf16[256,128,128]{2,1,0:T(8,128)(2,1)}, /*inde...) while((s32[]{:T(128)}, f32[32,128,512]{2,1,0:T(8,128)}, ...), condition=%wide.region_3.5_spmd, body=%wide.region_1.0_spmd.sunk | while | flops 1086326400 | bytes 94382912 | solution.py:50
  699.1 0.7 dynamic_slice.38
  700.4 0.1 dynamic_slice.39
  700.5 0.1 fusion.19
  700.6 0.1 and_bitcast_fusion.2
  700.7 8.0 gather_fusion
  708.7 12.2 %convolution_multiply_fusion.2 = f32[64,128,512]{2,1,0:T(8,128)} fusion(f32[64]{0:T(128)S(1)} %dynamic_slice.39, bf16[64,128,512]{2,1,0:T(8,128)(2,1)} %gather_fusion, pred[64]{0:T(512)(128)(4,1)S(1)} %get-tuple-element.114, bf16[256,128,128]{2,1,0:T(8,128)(2,1)} %get-tuple-element.141, s32[]{:T(128)S(6)} %select_n.70), kind=kOutput, calls=%fused_computation.4.clone.1 | convolution fusion | flops 1082130432 | bytes 27263300 | tf_op jit(solution)/shard_map/while/body/eval_jaxpr/kab,kbw->kaw/dot_general | solution.py:45
  720.9 37.0 %scatter_fusion = f32[32,128,512]{2,1,0:T(8,128)} fusion(f32[32,128,512]{2,1,0:T(8,128)} %get-tuple-element.127, s32[64]{0:T(128)S(1)} %fusion.19, f32[64,128,512]{2,1,0:T(8,128)} %convolution_multiply_fusion.2), kind=kCustom, calls=%fused_computation.3.clone.1 | custom fusion | flops 4194304 | bytes 50331904 | tf_op jit(solution)/shard_map/while/body/eval_jaxpr/scatter-add | solution.py:46
  757.9 0.7 dynamic_slice.38
  759.2 0.1 dynamic_slice.39
  759.3 0.1 fusion.19
  759.4 0.1 and_bitcast_fusion.2
  759.5 8.0 gather_fusion
  767.4 12.2 %convolution_multiply_fusion.2 = f32[64,128,512]{2,1,0:T(8,128)} fusion(f32[64]{0:T(128)S(1)} %dynamic_slice.39, bf16[64,128,512]{2,1,0:T(8,128)(2,1)} %gather_fusion, pred[64]{0:T(512)(128)(4,1)S(1)} %get-tuple-element.114, bf16[256,128,128]{2,1,0:T(8,128)(2,1)} %get-tuple-element.141, s32[]{:T(128)S(6)} %select_n.70), kind=kOutput, calls=%fused_computation.4.clone.1 | convolution fusion | flops 1082130432 | bytes 27263300 | tf_op jit(solution)/shard_map/while/body/eval_jaxpr/kab,kbw->kaw/dot_general | solution.py:45
  779.6 36.5 %scatter_fusion = f32[32,128,512]{2,1,0:T(8,128)} fusion(f32[32,128,512]{2,1,0:T(8,128)} %get-tuple-element.127, s32[64]{0:T(128)S(1)} %fusion.19, f32[64,128,512]{2,1,0:T(8,128)} %convolution_multiply_fusion.2), kind=kCustom, calls=%fused_computation.3.clone.1 | custom fusion | flops 4194304 | bytes 50331904 | tf_op jit(solution)/shard_map/while/body/eval_jaxpr/scatter-add | solution.py:46
  816.1 0.7 dynamic_slice.38
  817.4 0.1 dynamic_slice.39
  817.5 0.1 fusion.19
  817.6 0.1 and_bitcast_fusion.2
  817.7 8.0 gather_fusion
  825.7 12.2 %convolution_multiply_fusion.2 = f32[64,128,512]{2,1,0:T(8,128)} fusion(f32[64]{0:T(128)S(1)} %dynamic_slice.39, bf16[64,128,512]{2,1,0:T(8,128)(2,1)} %gather_fusion, pred[64]{0:T(512)(128)(4,1)S(1)} %get-tuple-element.114, bf16[256,128,128]{2,1,0:T(8,128)(2,1)} %get-tuple-element.141, s32[]{:T(128)S(6)} %select_n.70), kind=kOutput, calls=%fused_computation.4.clone.1 | convolution fusion | flops 1082130432 | bytes 27263300 | tf_op jit(solution)/shard_map/while/body/eval_jaxpr/kab,kbw->kaw/dot_general | solution.py:45
  837.9 36.4 %scatter_fusion = f32[32,128,512]{2,1,0:T(8,128)} fusion(f32[32,128,512]{2,1,0:T(8,128)} %get-tuple-element.127, s32[64]{0:T(128)S(1)} %fusion.19, f32[64,128,512]{2,1,0:T(8,128)} %convolution_multiply_fusion.2), kind=kCustom, calls=%fused_computation.3.clone.1 | custom fusion | flops 4194304 | bytes 50331904 | tf_op jit(solution)/shard_map/while/body/eval_jaxpr/scatter-add | solution.py:46
  874.3 0.7 dynamic_slice.38
  875.6 0.1 dynamic_slice.39
  875.7 0.1 fusion.19
  875.8 0.1 and_bitcast_fusion.2
  875.9 8.0 gather_fusion
  883.9 12.2 %convolution_multiply_fusion.2 = f32[64,128,512]{2,1,0:T(8,128)} fusion(f32[64]{0:T(128)S(1)} %dynamic_slice.39, bf16[64,128,512]{2,1,0:T(8,128)(2,1)} %gather_fusion, pred[64]{0:T(512)(128)(4,1)S(1)} %get-tuple-element.114, bf16[256,128,128]{2,1,0:T(8,128)(2,1)} %get-tuple-element.141, s32[]{:T(128)S(6)} %select_n.70), kind=kOutput, calls=%fused_computation.4.clone.1 | convolution fusion | flops 1082130432 | bytes 27263300 | tf_op jit(solution)/shard_map/while/body/eval_jaxpr/kab,kbw->kaw/dot_general | solution.py:45
  896.1 36.4 %scatter_fusion = f32[32,128,512]{2,1,0:T(8,128)} fusion(f32[32,128,512]{2,1,0:T(8,128)} %get-tuple-element.127, s32[64]{0:T(128)S(1)} %fusion.19, f32[64,128,512]{2,1,0:T(8,128)} %convolution_multiply_fusion.2), kind=kCustom, calls=%fused_computation.3.clone.1 | custom fusion | flops 4194304 | bytes 50331904 | tf_op jit(solution)/shard_map/while/body/eval_jaxpr/scatter-add | solution.py:46
  932.5 4.2 convert_element_type.12
  936.6 0.4 copy-done
  937.0 3.4 fusion.9
  940.4 269.5 %all-reduce.2.cloned.1.call-done = f32[512,512]{1,0:T(8,128)} async-done(((f32[512,512]{1,0:T(8,128)}), f32[512,512]{1,0:T(8,128)}) %all-reduce.2.cloned.1.call-update) | async-done | bytes 1048592 | tf_op jit(solution)/shard_map/psum | solution.py:63
  1210.0 1.4 constant_dynamic-slice_fusion.2
  (25 shorter events, 0.1 us)
Async XLA Ops:
  6.5 2.3 copy-start.2
  6.5 650.8 %all-gather.3.cloned.1.call-start = ((), (), s32[]{:S(2)}) async-start(), calls=%async_computation.1 | async-start | bytes 37748736 | tf_op jit(solution)/shard_map/all_gather | solution.py:15
  8.8 1201.2 %all-reduce.2.cloned.1.call-start = ((), (), s32[]{:S(2)}) async-start(), calls=%async_computation | async-start | bytes 2097152 | tf_op jit(solution)/shard_map/psum | solution.py:63
  679.4 7.0 collective-permute-start
  683.2 7.7 collective-permute-start.1
  686.0 13.1 %copy-start.1 = (s32[256,2]{0,1:T(2,128)S(1)}, s32[256,2]{0,1:T(2,128)}, u32[]{:S(2)}) copy-start(s32[256,2]{0,1:T(2,128)} %param.11) | copy-start | bytes 6148
  932.5 4.6 copy-start
Sparse Core Ops, SparseCore 0:
  9.1 648.1 all-gather.2
  940.6 269.3 all-reduce.1
